TPU v7x, 32 devices: a whole 2x2x4 slice. The times are simulated.
32 devices in a mesh: pb: 8 (over y, x, core), row: 4 (over z).
Axes of the slice: x: 2, y: 2, z: 4, core: 2. Of those that a mesh axis runs over, the one named last changes fastest.
Arguments:
- valence_bands: bfloat16 [8, 20, 4096], P('pb', None, 'row'), may hold values from -0.75 to 0.75
- conduction_bands: bfloat16 [8, 20, 4096], P('pb', None, 'row'), may hold values from -6 to 6
- screened: bfloat16 [8, 4096, 4096], P('pb', 'row'), may hold values from -0.09375 to 0.09375
- pair_list: int32 [16, 2], replicated, may hold values from 0 to 7, as said below
- transfer_index: int32 [16, 1], replicated, may hold values from 0 to 7; in each aligned block of 16 rows (0 to 15, 16 to 31, ...) at most 6 rows name the same one
- owner_map: int32 [8], replicated, may hold values from 0 to 7, as said below
Outputs:
- direct: bfloat16 [16, 400, 400], P('pb', 'row')
- mirror: bfloat16 [16, 400, 400], P('pb', 'row')
Inputs may be any that keep to these rules, and one draw needn't show every extreme that they name: owner_map is a permutation of 0 to 7. `pair_list`: the two k-points of a pair differ. The first k-point of pairs e * 2 to e * 2 + 1 is the one that owner_map sends to e. Over all pairs, the second k-points are sent by owner_map to every value 0 to 7 exactly 2 times. `transfer_index`: at most 6 pairs share one momentum transfer, and some transfer has exactly 6; every transfer has at least one pair.
All inputs are finite; a program needn't handle non-finite values.
Results may differ from a plain program's by a relative error of at most 0.0065.
Values may be sent and summed in bfloat16 or wider, within the bound.
No kernel may reach another device: no remote copies, remote signals or barrier semaphores. Data moves between devices by JAX's collectives and lax.ppermute only.
A program may use at most 64 MiB of HBM per device.

v0:
```python
import jax
import jax.numpy as jnp
from jax import lax
from jax.sharding import PartitionSpec as P

PAIR_DEV = 2
MOST = 6


def rank_table(labels, groups, slots_per):
    total_rows = labels.shape[0]
    member = (labels[None, :] == jnp.arange(groups, dtype=jnp.int32)[:, None]).astype(jnp.int32)
    before = jnp.cumsum(member, axis=1) - 1
    placed = member[:, None, :] * (
        before[:, None, :] == jnp.arange(slots_per, dtype=jnp.int32)[None, :, None]
    ).astype(jnp.int32)
    numbers = jnp.arange(total_rows, dtype=jnp.int32) + 1
    return jnp.sum(placed * numbers[None, None, :], axis=2) - 1


def pair_kernel(val_first, val_second, con_first, con_second, screen_rows):
    val_count = val_first.shape[0]
    con_count = con_first.shape[0]
    val_pairs = val_first[:, None, :].astype(jnp.float32) * val_second[None, :, :].astype(
        jnp.float32
    )
    val_pairs = val_pairs.reshape(val_count * val_count, val_first.shape[1]).astype(jnp.bfloat16)
    con_pairs = con_first[:, None, :].astype(jnp.float32) * con_second[None, :, :].astype(
        jnp.float32
    )
    con_pairs = con_pairs.reshape(con_count * con_count, con_first.shape[1]).astype(jnp.bfloat16)
    interim = lax.dot_general(
        screen_rows, con_pairs, (((1,), (1,)), ((), ())), preferred_element_type=jnp.float32
    ).astype(jnp.bfloat16)
    partial_sum = jnp.dot(val_pairs, interim, preferred_element_type=jnp.float32)
    partial_sum = partial_sum.reshape(val_count, val_count, con_count, con_count).transpose(
        0, 2, 1, 3
    )
    return partial_sum.reshape(val_count * con_count, val_count * con_count)


def shards(valence_bands, conduction_bands, screened, pair_list, transfer_index, owner_map):
    groups = lax.axis_size("pb")
    rows_split = lax.axis_size("row")
    device = lax.axis_index("pb")
    val_all, con_local = (
        lax.all_gather(valence_bands, "pb", axis=0, tiled=True),
        lax.all_gather(conduction_bands, "pb", axis=0, tiled=True),
    )
    slot_table = rank_table(transfer_index[:, 0], groups, MOST)
    own_slots = lax.dynamic_index_in_dim(slot_table, device, 0, keepdims=False)
    live_pair = jnp.maximum(own_slots, 0)
    slot_first = jnp.take(owner_map, jnp.take(pair_list[:, 0], live_pair))
    slot_second = jnp.take(owner_map, jnp.take(pair_list[:, 1], live_pair))
    val_first = jnp.take(val_all, slot_first, axis=0)
    val_second = jnp.take(val_all, slot_second, axis=0)
    con_full = lax.all_gather(con_local, "row", axis=2, tiled=True)
    con_first = jnp.take(con_full, slot_first, axis=0)
    con_second = jnp.take(con_full, slot_second, axis=0)
    screen_rows = screened[0]

    def one_slot(operands):
        return pair_kernel(operands[0], operands[1], operands[2], operands[3], screen_rows)

    partials = lax.map(one_slot, (val_first, val_second, con_first, con_second))
    shares = lax.psum_scatter(partials, "row", scatter_dimension=1, tiled=True).astype(jnp.bfloat16)
    band_rows = shares.shape[1]
    mirror_table = rank_table(jnp.take(owner_map, pair_list[:, 1]), groups, PAIR_DEV)
    flat_slots = slot_table.reshape(-1)
    own_direct = device * PAIR_DEV + jnp.arange(PAIR_DEV, dtype=jnp.int32)
    own_mirror = lax.dynamic_index_in_dim(mirror_table, device, 0, keepdims=False)
    wanted = jnp.concatenate([own_direct, own_mirror])
    select = (wanted[:, None] == flat_slots[None, :]).astype(jnp.bfloat16)
    arrived = jnp.einsum(
        "ji,ixy->jxy",
        select,
        lax.all_gather(shares, "pb", axis=0, tiled=True),
        preferred_element_type=jnp.float32,
    )
    direct = arrived[:PAIR_DEV].astype(jnp.bfloat16)
    mirror_rows = arrived[PAIR_DEV:].astype(jnp.bfloat16)
    turned = jnp.transpose(mirror_rows, (0, 2, 1)).reshape(
        PAIR_DEV, rows_split, band_rows, band_rows
    )
    swapped = lax.all_to_all(turned, "row", split_axis=1, concat_axis=3, tiled=True)
    mirror = swapped.reshape(PAIR_DEV, band_rows, band_rows * rows_split)
    return (direct, mirror)


def solution(mesh):
    in_specs = (P("pb", None, "row"), P("pb", None, "row"), P("pb", "row", None), P(), P(), P())
    out_specs = (P("pb", "row", None), P("pb", "row", None))
    return jax.shard_map(shards, mesh=mesh, in_specs=in_specs, out_specs=out_specs, check_vma=False)
```

profile of v0, /device:TPU:0, one launch (start us, length us, event | category | flops | bytes accessed | tf_op | source)
XLA Modules:
  0.0 460.9 jit_solution(9152695233821279163)
XLA Ops:
  7.2 12.9 %all_gather.13 = bf16[8,20,1024]{2,1,0:T(8,128)(2,1)} all-gather(bf16[1,20,1024]{2,1,0:T(8,128)(2,1)} %param.17), channel_id=1, replica_groups=mesh['pb'=8,'row'=4] {'pb'}, dimensions={0}, use_global_device_ids=true | all-gather | bytes 368640 | tf_op jit(solution)/shard_map/all_gather | solution.py:48
  24.9 8.8 %all_gather.12 = bf16[8,20,1024]{2,1,0:T(8,128)(2,1)S(1)} all-gather(bf16[1,20,1024]{2,1,0:T(8,128)(2,1)} %param.16), channel_id=1, replica_groups=mesh['pb'=8,'row'=4] {'pb'}, dimensions={0}, use_global_device_ids=true | all-gather | bytes 368640 | tf_op jit(solution)/shard_map/all_gather | solution.py:47
  37.8 19.8 %all-gather.3.cloned.1.call-done = bf16[8,20,4096]{2,1,0:T(8,128)(2,1)} async-done(((bf16[8,20,1024]{2,1,0:T(8,128)(2,1)}), bf16[8,20,4096]{2,1,0:T(8,128)(2,1)}) %all-gather.3.cloned.1.call-update) | async-done | bytes 1310736 | tf_op jit(solution)/shard_map/all_gather | solution.py:57
  57.6 2.1 gather_fusion.8
  59.8 1.2 broadcast_select_fusion
  62.8 156.2 %while.10 = (s32[]{:T(128)}, f32[6,400,400]{1,2,0:T(8,128)}, bf16[6,20,1024]{2,1,0:T(8,128)(2,1)}, bf16[6,20,1024]{2,1,0:T(8,128)(2,1)}, bf16[6,20,4096]{2,1,0:T...) while((s32[]{:T(128)}, f32[6,400,400]{1,2,0:T(8,128)}, ...), condition=%wide.region_5.10_spmd, body=%wide.region_4.9_spmd.sunk | while | flops 3687833600 | bytes 31480412 | solution.py:65
  63.9 2.6 multiply_convert_fusion.3
  66.5 3.9 convert_element_type.89
  70.4 7.0 %convolution_convert_fusion.3 = bf16[400,1024]{1,0:T(8,128)(2,1)} fusion(bf16[400,4096]{1,0:T(8,128)(2,1)S(1)} %convert_element_type.89, bf16[1024,4096]{1,0:T(8,128)(2,1)} %get-tuple-element.156), kind=kOutput, calls=%fused_computation.12.clone.1 | convolution fusion | flops 3355852800 | bytes 12484608 | tf_op jit(solution)/shard_map/while/body/eval_jaxpr/dot_general | solution.py:32
  77.4 1.2 reshape.284
  79.5 4.5 convolution_bitcast_fusion.2
  84.0 3.6 broadcast_in_dim.75
  89.9 2.6 multiply_convert_fusion.3
  92.6 3.9 convert_element_type.89
  96.4 7.0 %convolution_convert_fusion.3 = bf16[400,1024]{1,0:T(8,128)(2,1)} fusion(bf16[400,4096]{1,0:T(8,128)(2,1)S(1)} %convert_element_type.89, bf16[1024,4096]{1,0:T(8,128)(2,1)} %get-tuple-element.156), kind=kOutput, calls=%fused_computation.12.clone.1 | convolution fusion | flops 3355852800 | bytes 12484608 | tf_op jit(solution)/shard_map/while/body/eval_jaxpr/dot_general | solution.py:32
  103.5 1.2 reshape.284
  105.6 4.5 convolution_bitcast_fusion.2
  110.0 3.6 broadcast_in_dim.75
  116.0 2.6 multiply_convert_fusion.3
  118.6 3.9 convert_element_type.89
  122.5 7.0 %convolution_convert_fusion.3 = bf16[400,1024]{1,0:T(8,128)(2,1)} fusion(bf16[400,4096]{1,0:T(8,128)(2,1)S(1)} %convert_element_type.89, bf16[1024,4096]{1,0:T(8,128)(2,1)} %get-tuple-element.156), kind=kOutput, calls=%fused_computation.12.clone.1 | convolution fusion | flops 3355852800 | bytes 12484608 | tf_op jit(solution)/shard_map/while/body/eval_jaxpr/dot_general | solution.py:32
  129.5 1.2 reshape.284
  131.6 4.5 convolution_bitcast_fusion.2
  136.0 3.6 broadcast_in_dim.75
  142.0 2.6 multiply_convert_fusion.3
  144.6 3.9 convert_element_type.89
  148.5 7.0 %convolution_convert_fusion.3 = bf16[400,1024]{1,0:T(8,128)(2,1)} fusion(bf16[400,4096]{1,0:T(8,128)(2,1)S(1)} %convert_element_type.89, bf16[1024,4096]{1,0:T(8,128)(2,1)} %get-tuple-element.156), kind=kOutput, calls=%fused_computation.12.clone.1 | convolution fusion | flops 3355852800 | bytes 12484608 | tf_op jit(solution)/shard_map/while/body/eval_jaxpr/dot_general | solution.py:32
  155.5 1.2 reshape.284
  157.6 4.5 convolution_bitcast_fusion.2
  162.1 3.6 broadcast_in_dim.75
  168.0 2.6 multiply_convert_fusion.3
  170.6 3.9 convert_element_type.89
  174.5 7.0 %convolution_convert_fusion.3 = bf16[400,1024]{1,0:T(8,128)(2,1)} fusion(bf16[400,4096]{1,0:T(8,128)(2,1)S(1)} %convert_element_type.89, bf16[1024,4096]{1,0:T(8,128)(2,1)} %get-tuple-element.156), kind=kOutput, calls=%fused_computation.12.clone.1 | convolution fusion | flops 3355852800 | bytes 12484608 | tf_op jit(solution)/shard_map/while/body/eval_jaxpr/dot_general | solution.py:32
  181.6 1.2 reshape.284
  183.7 4.5 convolution_bitcast_fusion.2
  188.1 3.6 broadcast_in_dim.75
  194.0 2.6 multiply_convert_fusion.3
  196.7 3.9 convert_element_type.89
  200.5 7.0 %convolution_convert_fusion.3 = bf16[400,1024]{1,0:T(8,128)(2,1)} fusion(bf16[400,4096]{1,0:T(8,128)(2,1)S(1)} %convert_element_type.89, bf16[1024,4096]{1,0:T(8,128)(2,1)} %get-tuple-element.156), kind=kOutput, calls=%fused_computation.12.clone.1 | convolution fusion | flops 3355852800 | bytes 12484608 | tf_op jit(solution)/shard_map/while/body/eval_jaxpr/dot_general | solution.py:32
  207.6 1.2 reshape.284
  209.7 4.5 convolution_bitcast_fusion.2
  214.1 3.6 broadcast_in_dim.75
  219.0 169.8 %all-reduce.2 = bf16[6,400,400]{1,2,0:T(8,128)(2,1)S(1)} all-reduce(f32[6,400,400]{1,2,0:T(8,128)} %get-tuple-element.43), channel_id=2, replica_groups=mesh['pb'=8,'row'=4] {'row'}, use_global_device_ids=true, to_apply=%region_6.11.clone | all-reduce | flops 960000 | bytes 5760000
  391.4 36.1 %all-gather.5.cloned.1.call-done = bf16[48,100,400]{1,2,0:T(8,128)(2,1)} async-done(((bf16[6,100,400]{1,2,0:T(8,128)(2,1)}), bf16[48,100,400]{1,2,0:T(8,128)(2,1)}) %all-gather.5.cloned.1.call-update) | async-done | bytes 3840016 | tf_op jit(solution)/shard_map/all_gather | solution.py:77
  427.5 8.4 %copy.27 = bf16[48,100,400]{2,0,1:T(8,128)(2,1)} copy(bf16[48,100,400]{1,2,0:T(8,128)(2,1)} %all-gather.5.cloned.1.call-done) | data formatting | bytes 7680000 | tf_op jit(solution)/shard_map/all_gather | solution.py:77
  435.9 3.2 convolution_convert_fusion.1
  440.4 12.5 %all_to_all.15 = bf16[2,4,100,100]{2,0,3,1:T(2,128)(2,1)S(1)} all-to-all(bf16[2,4,100,100]{2,0,3,1:T(2,128)(2,1)S(1)} %copy.28), channel_id=1, replica_groups=mesh['pb'=8,'row'=4] {'row'}, dimensions={1} | all-to-all | bytes 320000 | tf_op jit(solution)/shard_map/all_to_all | solution.py:85
  452.9 1.2 copy.29
  (81 shorter events, 32.8 us)
Async XLA Ops:
  7.2 16.4 %copy-start = (s32[8]{0:T(128)S(1)}, s32[8]{0:T(128)}, u32[]{:S(2)}) copy-start(s32[8]{0:T(128)} %param.21) | copy-start | bytes 100
  7.2 27.8 %copy-start.3 = (u32[32]{0:T(128)S(1)}, u32[32]{0:T(128)}, u32[]{:S(2)}) copy-start(u32[32]{0:T(128)} %constant.110) | copy-start | bytes 388
  7.2 50.4 %all-gather.3.cloned.1.call-start = ((), (), s32[]{:S(2)}) async-start(), calls=%async_computation.1 | async-start | bytes 1966080 | tf_op jit(solution)/shard_map/all_gather | solution.py:57
  20.2 407.3 %all-gather.5.cloned.1.call-start = ((), (), s32[]{:S(2)}) async-start(), calls=%async_computation.2 | async-start | bytes 5529600 | tf_op jit(solution)/shard_map/all_gather | solution.py:77
  57.6 3.4 copy-start.1
  219.0 171.7 %copy-start.2 = (s32[16,2]{0,1:T(2,128)S(1)}, s32[16,2]{0,1:T(2,128)}, u32[]{:S(2)}) copy-start(s32[16,2]{0,1:T(2,128)} %param.19) | copy-start | bytes 388
Sparse Core Ops, SparseCore 0:
  20.3 37.2 all-gather.2
  390.1 37.3 all-gather.4
where the time goes:
time: 463 us; the launch traced here: 461 us
  blocking collectives  204 us (44%)
  local copies, waits for them, and re-layouts  80 us (17%)
  matrix products  72.2 us (16%)
  waiting for transfers between devices  55.9 us (12%)
  other arithmetic  33.6 us (7%)
  between operations  14.9 us (3%)
    unnamed x1, blocking collectives  170 us
    dot_general x6, matrix products, pair_kernel(): lax.dot_general(screen_rows, con_pairs, (((1,), (1,)), ((), ())), preferr...  42.1 us
    all_gather x1, waiting for transfers between devices, shards(): lax.all_gather(shares, 'pb', axis=0, tiled=True)  36.1 us
    dot_general x6, matrix products, pair_kernel(): jnp.dot(val_pairs, interim, preferred_element_type=jnp.float32)  26.8 us
    convert_element_type x6, local copies, waits for them, and re-layouts, pair_kernel(): con_pairs.reshape(con_count * con_count, con_first.shape[1])  23.3 us
    broadcast_in_dim x6, local copies, waits for them, and re-layouts, shards(): partials = lax.map(one_slot, (val_first, val_second, con_first, con_second))  21.6 us
    all_gather x1, waiting for transfers between devices, shards(): con_full = lax.all_gather(con_local, 'row', axis=2, tiled=True)  19.8 us
    convert_element_type x6, other arithmetic, pair_kernel(): con_pairs.reshape(con_count * con_count, con_first.shape[1])  15.6 us
  transfers between devices with their start and end apart: 2, of which 2 were waited for; matrix products, arithmetic and copies ran while one was open for 2% of the time, Pallas kernels for 0%

commit v1 on v0

--- a/solution.py
+++ b/solution.py
@@ -5,6 +5,21 @@
 
 PAIR_DEV = 2
 MOST = 6
+
+
+def save_arrays_up(arr_in, out_dim, row_data):
+    y2 = lax.axis_size("pb")
+    reached, step_out, near = (y2, lax.axis_index("pb"), arr_in.shape[out_dim])
+    all_blocks = []
+    for s in range(reached):
+        all_blocks.append((s, (s + 1) % reached))
+    after, tile_out = (arr_in, None)
+    for k in range(reached):
+        local_now = lax.ppermute(after, "pb", all_blocks) if k < reached - 1 else None
+        long_array = row_data(after, (step_out - k) % reached * near)
+        tile_out = long_array if tile_out is None else tile_out + long_array
+        after = local_now
+    return tile_out
 
 
 def rank_table(labels, groups, slots_per):
@@ -71,11 +86,15 @@
     own_mirror = lax.dynamic_index_in_dim(mirror_table, device, 0, keepdims=False)
     wanted = jnp.concatenate([own_direct, own_mirror])
     select = (wanted[:, None] == flat_slots[None, :]).astype(jnp.bfloat16)
-    arrived = jnp.einsum(
-        "ji,ixy->jxy",
-        select,
-        lax.all_gather(shares, "pb", axis=0, tiled=True),
-        preferred_element_type=jnp.float32,
+    arrived = save_arrays_up(
+        shares,
+        0,
+        lambda shard, start: jnp.einsum(
+            "ji,ixy->jxy",
+            lax.dynamic_slice_in_dim(select, start, shard.shape[0], axis=1),
+            shard,
+            preferred_element_type=jnp.float32,
+        ),
     )
     direct = arrived[:PAIR_DEV].astype(jnp.bfloat16)
     mirror_rows = arrived[PAIR_DEV:].astype(jnp.bfloat16)

time: 463 us -> 486 us (1.050)
  waiting for transfers between devices: 55.9 us -> 77.2 us
  local copies, waits for them, and re-layouts: 80 us -> 85.2 us
    ppermute x0 -> x7, waiting for transfers between devices: none -> 57.2 us  [save_arrays_up(): lax.ppermute(after, 'pb', all_blocks)]
    all_gather x1 -> x0, waiting for transfers between devices: 36.1 us -> none  [shards(): lax.all_gather(shares, 'pb', axis=0, tiled=True)]
    ppermute x0 -> x7, local copies, waits for them, and re-layouts: none -> 13.2 us  [save_arrays_up(): lax.ppermute(after, 'pb', all_blocks)]
    all_gather x1 -> x0, local copies, waits for them, and re-layouts: 8.41 us -> none  [shards(): lax.all_gather(shares, 'pb', axis=0, tiled=True)]
  transfers between devices with their start and end apart: 2 -> 8, of which waited for: 2 -> 8; matrix products, arithmetic and copies ran while one was open for 2% -> 5% of each run, Pallas kernels for 0% -> 0%
where the time goes in v1:
time: 486 us; the launch traced here: 484 us
  blocking collectives  200 us (41%)
  local copies, waits for them, and re-layouts  85.2 us (18%)
  waiting for transfers between devices  77.2 us (16%)
  matrix products  72.7 us (15%)
  other arithmetic  33.7 us (7%)
  between operations  15.2 us (3%)
    unnamed x1, blocking collectives  169 us
    ppermute x7, waiting for transfers between devices, save_arrays_up(): lax.ppermute(after, 'pb', all_blocks)  57.2 us
    dot_general x6, matrix products, pair_kernel(): lax.dot_general(screen_rows, con_pairs, (((1,), (1,)), ((), ())), preferr...  42.2 us
    dot_general x6, matrix products, pair_kernel(): jnp.dot(val_pairs, interim, preferred_element_type=jnp.float32)  27 us
    convert_element_type x6, local copies, waits for them, and re-layouts, pair_kernel(): con_pairs.reshape(con_count * con_count, con_first.shape[1])  23.3 us
    broadcast_in_dim x6, local copies, waits for them, and re-layouts, shards(): partials = lax.map(one_slot, (val_first, val_second, con_first, con_second))  21.6 us
    all_gather x1, waiting for transfers between devices, shards(): con_full = lax.all_gather(con_local, 'row', axis=2, tiled=True)  20 us
    convert_element_type x6, other arithmetic, pair_kernel(): con_pairs.reshape(con_count * con_count, con_first.shape[1])  15.6 us
  transfers between devices with their start and end apart: 8, of which 8 were waited for; matrix products, arithmetic and copies ran while one was open for 5% of the time, Pallas kernels for 0%

profile of v1, /device:TPU:0, one launch (start us, length us, event | category | flops | bytes accessed | tf_op | source)
XLA Modules:
  0.0 484.3 jit_solution(7427244148462633927)
XLA Ops:
  7.2 12.9 %all_gather.10 = bf16[8,20,1024]{2,1,0:T(8,128)(2,1)} all-gather(bf16[1,20,1024]{2,1,0:T(8,128)(2,1)} %param.17), channel_id=1, replica_groups=mesh['pb'=8,'row'=4] {'pb'}, dimensions={0}, use_global_device_ids=true | all-gather | bytes 368640 | tf_op jit(solution)/shard_map/all_gather | solution.py:63
  24.9 8.7 %all_gather.9 = bf16[8,20,1024]{2,1,0:T(8,128)(2,1)S(1)} all-gather(bf16[1,20,1024]{2,1,0:T(8,128)(2,1)S(1)} %copy-done.5), channel_id=1, replica_groups=mesh['pb'=8,'row'=4] {'pb'}, dimensions={0}, use_global_device_ids=true | all-gather | bytes 368640 | tf_op jit(solution)/shard_map/all_gather | solution.py:62
  37.6 20.0 %all-gather.2.cloned.1.call-done = bf16[8,20,4096]{2,1,0:T(8,128)(2,1)} async-done(((bf16[8,20,1024]{2,1,0:T(8,128)(2,1)}), bf16[8,20,4096]{2,1,0:T(8,128)(2,1)}) %all-gather.2.cloned.1.call-update) | async-done | bytes 1310736 | tf_op jit(solution)/shard_map/all_gather | solution.py:72
  57.6 2.1 gather_fusion.8
  62.8 156.4 %while.10 = (s32[]{:T(128)}, f32[6,400,400]{1,2,0:T(8,128)}, bf16[6,20,1024]{2,1,0:T(8,128)(2,1)}, bf16[6,20,1024]{2,1,0:T(8,128)(2,1)}, bf16[6,20,4096]{2,1,0:T...) while((s32[]{:T(128)}, f32[6,400,400]{1,2,0:T(8,128)}, ...), condition=%wide.region_5.10_spmd, body=%wide.region_4.9_spmd.sunk | while | flops 3687833600 | bytes 31480412 | solution.py:80
  63.9 2.6 multiply_convert_fusion.3
  66.5 3.9 convert_element_type.89
  70.4 7.0 %convolution_convert_fusion.2 = bf16[400,1024]{1,0:T(8,128)(2,1)} fusion(bf16[400,4096]{1,0:T(8,128)(2,1)S(1)} %convert_element_type.89, bf16[1024,4096]{1,0:T(8,128)(2,1)} %get-tuple-element.156), kind=kOutput, calls=%fused_computation.12.clone.1 | convolution fusion | flops 3355852800 | bytes 12484608 | tf_op jit(solution)/shard_map/while/body/eval_jaxpr/dot_general | solution.py:47
  79.5 4.5 convolution_bitcast_fusion.2
  84.0 3.6 broadcast_in_dim.75
  90.0 2.6 multiply_convert_fusion.3
  92.6 3.9 convert_element_type.89
  96.5 7.0 %convolution_convert_fusion.2 = bf16[400,1024]{1,0:T(8,128)(2,1)} fusion(bf16[400,4096]{1,0:T(8,128)(2,1)S(1)} %convert_element_type.89, bf16[1024,4096]{1,0:T(8,128)(2,1)} %get-tuple-element.156), kind=kOutput, calls=%fused_computation.12.clone.1 | convolution fusion | flops 3355852800 | bytes 12484608 | tf_op jit(solution)/shard_map/while/body/eval_jaxpr/dot_general | solution.py:47
  105.6 4.5 convolution_bitcast_fusion.2
  110.1 3.6 broadcast_in_dim.75
  116.0 2.6 multiply_convert_fusion.3
  118.7 3.9 convert_element_type.89
  122.5 7.0 %convolution_convert_fusion.2 = bf16[400,1024]{1,0:T(8,128)(2,1)} fusion(bf16[400,4096]{1,0:T(8,128)(2,1)S(1)} %convert_element_type.89, bf16[1024,4096]{1,0:T(8,128)(2,1)} %get-tuple-element.156), kind=kOutput, calls=%fused_computation.12.clone.1 | convolution fusion | flops 3355852800 | bytes 12484608 | tf_op jit(solution)/shard_map/while/body/eval_jaxpr/dot_general | solution.py:47
  131.7 4.5 convolution_bitcast_fusion.2
  136.2 3.6 broadcast_in_dim.75
  142.1 2.6 multiply_convert_fusion.3
  144.7 3.9 convert_element_type.89
  148.6 7.0 %convolution_convert_fusion.2 = bf16[400,1024]{1,0:T(8,128)(2,1)} fusion(bf16[400,4096]{1,0:T(8,128)(2,1)S(1)} %convert_element_type.89, bf16[1024,4096]{1,0:T(8,128)(2,1)} %get-tuple-element.156), kind=kOutput, calls=%fused_computation.12.clone.1 | convolution fusion | flops 3355852800 | bytes 12484608 | tf_op jit(solution)/shard_map/while/body/eval_jaxpr/dot_general | solution.py:47
  157.7 4.5 convolution_bitcast_fusion.2
  162.2 3.6 broadcast_in_dim.75
  168.1 2.6 multiply_convert_fusion.3
  170.7 3.9 convert_element_type.89
  174.6 7.0 %convolution_convert_fusion.2 = bf16[400,1024]{1,0:T(8,128)(2,1)} fusion(bf16[400,4096]{1,0:T(8,128)(2,1)S(1)} %convert_element_type.89, bf16[1024,4096]{1,0:T(8,128)(2,1)} %get-tuple-element.156), kind=kOutput, calls=%fused_computation.12.clone.1 | convolution fusion | flops 3355852800 | bytes 12484608 | tf_op jit(solution)/shard_map/while/body/eval_jaxpr/dot_general | solution.py:47
  183.8 4.5 convolution_bitcast_fusion.2
  188.3 3.6 broadcast_in_dim.75
  194.2 2.6 multiply_convert_fusion.3
  196.8 3.9 convert_element_type.89
  200.7 7.0 %convolution_convert_fusion.2 = bf16[400,1024]{1,0:T(8,128)(2,1)} fusion(bf16[400,4096]{1,0:T(8,128)(2,1)S(1)} %convert_element_type.89, bf16[1024,4096]{1,0:T(8,128)(2,1)} %get-tuple-element.156), kind=kOutput, calls=%fused_computation.12.clone.1 | convolution fusion | flops 3355852800 | bytes 12484608 | tf_op jit(solution)/shard_map/while/body/eval_jaxpr/dot_general | solution.py:47
  209.8 4.5 convolution_bitcast_fusion.2
  214.3 3.6 broadcast_in_dim.75
  219.2 169.3 %all-reduce.2 = bf16[6,400,400]{1,2,0:T(8,128)(2,1)S(1)} all-reduce(f32[6,400,400]{1,2,0:T(8,128)} %get-tuple-element.43), channel_id=2, replica_groups=mesh['pb'=8,'row'=4] {'row'}, use_global_device_ids=true, to_apply=%region_6.11.clone | all-reduce | flops 960000 | bytes 5760000
  389.5 9.8 %collective-permute-done = bf16[6,100,400]{1,2,0:T(8,128)(2,1)S(1)} collective-permute-done((bf16[6,100,400]{1,2,0:T(8,128)(2,1)S(1)}, bf16[6,100,400]{1,2,0:T(8,128)(2,1)S(1)}, u32[]{:S(2)}, u32[]{:S(2)}) %collective-permute-start) | collective-permute-done | bytes 480032 | tf_op jit(solution)/shard_map/ppermute | solution.py:18
  399.5 10.3 %collective-permute-done.1 = bf16[6,100,400]{1,2,0:T(8,128)(2,1)S(1)} collective-permute-done((bf16[6,100,400]{1,2,0:T(8,128)(2,1)S(1)}, bf16[6,100,400]{1,2,0:T(8,128)(2,1)S(1)}, u32[]{:S(2)}, u32[]{:S(2)}) %collective-permute-start.1) | collective-permute-done | bytes 480032 | tf_op jit(solution)/shard_map/ppermute | solution.py:18
  410.4 9.9 %collective-permute-done.2 = bf16[6,100,400]{1,2,0:T(8,128)(2,1)} collective-permute-done((bf16[6,100,400]{1,2,0:T(8,128)(2,1)S(1)}, bf16[6,100,400]{1,2,0:T(8,128)(2,1)}, u32[]{:S(2)}, u32[]{:S(2)}) %collective-permute-start.2) | collective-permute-done | bytes 480032 | tf_op jit(solution)/shard_map/ppermute | solution.py:18
  422.1 2.2 copy.49
  424.3 6.8 %collective-permute-done.3 = bf16[6,100,400]{1,2,0:T(8,128)(2,1)} collective-permute-done((bf16[6,100,400]{1,2,0:T(8,128)(2,1)}, bf16[6,100,400]{1,2,0:T(8,128)(2,1)}, u32[]{:S(2)}, u32[]{:S(2)}) %collective-permute-start.3) | collective-permute-done | bytes 480032 | tf_op jit(solution)/shard_map/ppermute | solution.py:18
  433.2 2.1 copy.51
  435.4 6.5 %collective-permute-done.4 = bf16[6,100,400]{1,2,0:T(8,128)(2,1)} collective-permute-done((bf16[6,100,400]{1,2,0:T(8,128)(2,1)}, bf16[6,100,400]{1,2,0:T(8,128)(2,1)}, u32[]{:S(2)}, u32[]{:S(2)}) %collective-permute-start.4) | collective-permute-done | bytes 480032 | tf_op jit(solution)/shard_map/ppermute | solution.py:18
  442.3 2.1 copy.52
  444.9 2.1 copy.53
  447.1 5.5 %collective-permute-done.5 = bf16[6,100,400]{1,2,0:T(8,128)(2,1)S(1)} collective-permute-done((bf16[6,100,400]{1,2,0:T(8,128)(2,1)}, bf16[6,100,400]{1,2,0:T(8,128)(2,1)S(1)}, u32[]{:S(2)}, u32[]{:S(2)}) %collective-permute-start.5) | collective-permute-done | bytes 480032 | tf_op jit(solution)/shard_map/ppermute | solution.py:18
  454.7 8.5 %collective-permute-done.6 = bf16[6,100,400]{1,2,0:T(8,128)(2,1)} collective-permute-done((bf16[6,100,400]{1,2,0:T(8,128)(2,1)S(1)}, bf16[6,100,400]{1,2,0:T(8,128)(2,1)}, u32[]{:S(2)}, u32[]{:S(2)}) %collective-permute-start.6) | collective-permute-done | bytes 480032 | tf_op jit(solution)/shard_map/ppermute | solution.py:18
  467.1 9.2 %all_to_all.15 = bf16[2,4,100,100]{2,0,3,1:T(2,128)(2,1)S(1)} all-to-all(bf16[2,4,100,100]{2,0,3,1:T(2,128)(2,1)S(1)} %copy.56), channel_id=1, replica_groups=mesh['pb'=8,'row'=4] {'row'}, dimensions={1} | all-to-all | bytes 320000 | tf_op jit(solution)/shard_map/all_to_all | solution.py:104
  (115 shorter events, 51.3 us)
Async XLA Ops:
  7.2 16.4 %copy-start = (s32[8]{0:T(128)S(1)}, s32[8]{0:T(128)}, u32[]{:S(2)}) copy-start(s32[8]{0:T(128)} %param.21) | copy-start | bytes 100
  7.2 17.7 %copy-start.5 = (bf16[1,20,1024]{2,1,0:T(8,128)(2,1)S(1)}, bf16[1,20,1024]{2,1,0:T(8,128)(2,1)}, u32[]{:S(2)}) copy-start(bf16[1,20,1024]{2,1,0:T(8,128)(2,1)} %param.16) | copy-start | bytes 122884
  7.2 50.4 %all-gather.2.cloned.1.call-start = ((), (), s32[]{:S(2)}) async-start(), calls=%async_computation.1 | async-start | bytes 1966080 | tf_op jit(solution)/shard_map/all_gather | solution.py:72
  20.2 14.5 %copy-start.7 = (u32[32]{0:T(128)S(1)}, u32[32]{0:T(128)}, u32[]{:S(2)}) copy-start(u32[32]{0:T(128)} %constant.170) | copy-start | bytes 388
  57.6 3.4 copy-start.1
  219.2 180.1 %copy-start.6 = (s32[16,2]{0,1:T(2,128)S(1)}, s32[16,2]{0,1:T(2,128)}, u32[]{:S(2)}) copy-start(s32[16,2]{0,1:T(2,128)} %param.19) | copy-start | bytes 388
  388.7 10.5 %collective-permute-start = (bf16[6,100,400]{1,2,0:T(8,128)(2,1)S(1)}, bf16[6,100,400]{1,2,0:T(8,128)(2,1)S(1)}, u32[]{:S(2)}, u32[]{:S(2)}) collective-permute-start(bf16[6,100,400]{1,2,0:T(8,128)(2,1)S(1)} %dynamic-slice_convert_fusion), channel_id=1, source_target_pairs={{0,4},{4,8},{8,12},{12,16},{16,20},{20,24},{24,28},{28,0},{1,5},{5... | collective-permute-start | bytes 1440008 | tf_op jit(solution)/shard_map/ppermute | solution.py:18
  399.3 21.1 %copy-start.4 = (bf16[6,100,400]{1,2,0:T(8,128)(2,1)}, bf16[6,100,400]{1,2,0:T(8,128)(2,1)S(1)}, u32[]{:S(2)}) copy-start(bf16[6,100,400]{1,2,0:T(8,128)(2,1)S(1)} %collective-permute-done) | copy-start | bytes 1440004
  399.3 10.5 %collective-permute-start.1 = (bf16[6,100,400]{1,2,0:T(8,128)(2,1)S(1)}, bf16[6,100,400]{1,2,0:T(8,128)(2,1)S(1)}, u32[]{:S(2)}, u32[]{:S(2)}) collective-permute-start(bf16[6,100,400]{1,2,0:T(8,128)(2,1)S(1)} %collective-permute-done), channel_id=1, source_target_pairs={{0,4},{4,8},{8,12},{12,16},{16,20},{20,24},{24,28},{28,0},{1,5},{5... | collective-permute-start | bytes 1440008 | tf_op jit(solution)/shard_map/ppermute | solution.py:18
  409.7 10.7 %copy-start.2 = (bf16[6,100,400]{1,2,0:T(8,128)(2,1)}, bf16[6,100,400]{1,2,0:T(8,128)(2,1)S(1)}, u32[]{:S(2)}) copy-start(bf16[6,100,400]{1,2,0:T(8,128)(2,1)S(1)} %collective-permute-done.1) | copy-start | bytes 1440004
  409.7 10.6 %collective-permute-start.2 = (bf16[6,100,400]{1,2,0:T(8,128)(2,1)S(1)}, bf16[6,100,400]{1,2,0:T(8,128)(2,1)}, u32[]{:S(2)}, u32[]{:S(2)}) collective-permute-start(bf16[6,100,400]{1,2,0:T(8,128)(2,1)S(1)} %collective-permute-done.1), channel_id=1, source_target_pairs={{0,4},{4,8},{8,12},{12,16},{16,20},{20,24},{24,28},{28,0},{1,5},{5... | collective-permute-start | bytes 1440008 | tf_op jit(solution)/shard_map/ppermute | solution.py:18
  420.3 10.8 %collective-permute-start.3 = (bf16[6,100,400]{1,2,0:T(8,128)(2,1)}, bf16[6,100,400]{1,2,0:T(8,128)(2,1)}, u32[]{:S(2)}, u32[]{:S(2)}) collective-permute-start(bf16[6,100,400]{1,2,0:T(8,128)(2,1)} %collective-permute-done.2), channel_id=1, source_target_pairs={{0,4},{4,8},{8,12},{12,16},{16,20},{20,24},{24,28},{28,0},{1,5},{5... | collective-permute-start | bytes 1440008 | tf_op jit(solution)/shard_map/ppermute | solution.py:18
  422.0 9.5 %copy-start.3 = (bf16[6,100,400]{1,2,0:T(8,128)(2,1)S(1)}, bf16[6,100,400]{1,2,0:T(8,128)(2,1)}, u32[]{:S(2)}) copy-start(bf16[6,100,400]{1,2,0:T(8,128)(2,1)} %copy-done.2) | copy-start | bytes 1440004
  431.1 10.8 %collective-permute-start.4 = (bf16[6,100,400]{1,2,0:T(8,128)(2,1)}, bf16[6,100,400]{1,2,0:T(8,128)(2,1)}, u32[]{:S(2)}, u32[]{:S(2)}) collective-permute-start(bf16[6,100,400]{1,2,0:T(8,128)(2,1)} %collective-permute-done.3), channel_id=1, source_target_pairs={{0,4},{4,8},{8,12},{12,16},{16,20},{20,24},{24,28},{28,0},{1,5},{5... | collective-permute-start | bytes 1440008 | tf_op jit(solution)/shard_map/ppermute | solution.py:18
  441.9 10.7 %collective-permute-start.5 = (bf16[6,100,400]{1,2,0:T(8,128)(2,1)}, bf16[6,100,400]{1,2,0:T(8,128)(2,1)S(1)}, u32[]{:S(2)}, u32[]{:S(2)}) collective-permute-start(bf16[6,100,400]{1,2,0:T(8,128)(2,1)} %collective-permute-done.4), channel_id=1, source_target_pairs={{0,4},{4,8},{8,12},{12,16},{16,20},{20,24},{24,28},{28,0},{1,5},{5... | collective-permute-start | bytes 1440008 | tf_op jit(solution)/shard_map/ppermute | solution.py:18
  452.6 10.6 %collective-permute-start.6 = (bf16[6,100,400]{1,2,0:T(8,128)(2,1)S(1)}, bf16[6,100,400]{1,2,0:T(8,128)(2,1)}, u32[]{:S(2)}, u32[]{:S(2)}) collective-permute-start(bf16[6,100,400]{1,2,0:T(8,128)(2,1)S(1)} %collective-permute-done.5), channel_id=1, source_target_pairs={{0,4},{4,8},{8,12},{12,16},{16,20},{20,24},{24,28},{28,0},{1,5},{5... | collective-permute-start | bytes 1440008 | tf_op jit(solution)/shard_map/ppermute | solution.py:18
Sparse Core Ops, SparseCore 0:
  20.3 37.2 all-gather.1
